TPU v7x, 256 devices: a whole 4x4x8 slice. The times are simulated.
256 devices in a mesh: ctx: 64 (over y_lo, x, z), head: 4 (over y_hi, core).
Axes of the slice: x: 4, y: 4 (y_hi: 2, y_lo: 2; y = y_hi * 2 + y_lo), z: 8, core: 2. Of those that a mesh axis runs over, the one named last changes fastest.
Arguments:
- queries: bfloat16 [12288, 768], P(('ctx', 'head')), may hold values from -2.5 to 2.5
- keys: bfloat16 [12288, 768], P(('ctx', 'head')), may hold values from -2.5 to 2.5
- values: bfloat16 [12288, 768], P(('ctx', 'head')), may hold values from -6 to 6
- attended: bfloat16 [12288, 768], P(('ctx', 'head')), may hold values from -6 to 6
- grad_out: bfloat16 [12288, 768], P(('ctx', 'head')), may hold values from -6 to 6
- logsumexp: float32 [12288, 12], P('ctx', 'head'), may hold values from 5 to 8
Outputs:
- grad_queries: bfloat16 [12288, 768], P(('ctx', 'head'))
- grad_keys: bfloat16 [12288, 768], P(('ctx', 'head'))
- grad_values: bfloat16 [12288, 768], P(('ctx', 'head'))
All inputs are finite; a program needn't handle non-finite values.
Results may differ from a plain program's by a relative error of at most 0.0051.
Values may be sent and summed in bfloat16 or wider, within the bound.
A program may use at most 128 MiB of HBM per device.

v0:
```python
import jax
import jax.numpy as jnp
from jax import lax
from jax.sharding import PartitionSpec as P


def block_rows(length):
    for candidate in (2048, 1024, 512):
        return candidate
    return length


def over_blocks(advance, totals, tensors):
    length = tensors[0].shape[0]
    block_size = block_rows(length)
    stacked = tuple(
        (
            matrix.reshape((length // block_size, block_size) + matrix.shape[1:])
            for matrix in tensors
        )
    )

    def single(current, blocks):
        return (advance(current, blocks), None)

    return lax.scan(single, totals, stacked)[0]


def attend(query_part, grad_part, norm_part, delta_part, key_part, value_part, scaling):
    scores = (
        jnp.einsum("ahd,bhd->hab", query_part, key_part, preferred_element_type=jnp.float32)
        * scaling
    )
    weights = jnp.exp(scores - jnp.transpose(norm_part)[:, :, None])
    weights_low = weights.astype(jnp.bfloat16)
    dweights = jnp.einsum("ahd,bhd->hab", grad_part, value_part, preferred_element_type=jnp.float32)
    dscores = (weights * (dweights - jnp.transpose(delta_part)[:, :, None])).astype(jnp.bfloat16)
    return (weights_low, dscores)


def query_term(dscores, key_part, scaling):
    return (
        jnp.einsum("hab,bhd->ahd", dscores, key_part, preferred_element_type=jnp.float32) * scaling
    )


def key_terms(weights_low, dscores, query_part, grad_part, scaling):
    grad_key = (
        jnp.einsum("hab,ahd->bhd", dscores, query_part, preferred_element_type=jnp.float32)
        * scaling
    )
    grad_value = jnp.einsum(
        "hab,ahd->bhd", weights_low, grad_part, preferred_element_type=jnp.float32
    )
    return (grad_key, grad_value)


def local(queries, keys, values, attended, grad_out, logsumexp):
    heads_local = logsumexp.shape[1]
    group_size = lax.axis_size("head")
    width_local = queries.shape[1] // group_size
    head_width = width_local // heads_local
    scaling = head_width ** (-0.5)
    moved = (
        lax.all_to_all(queries, "head", split_axis=1, concat_axis=0, tiled=True),
        lax.all_to_all(keys, "head", split_axis=1, concat_axis=0, tiled=True),
        lax.all_to_all(values, "head", split_axis=1, concat_axis=0, tiled=True),
        lax.all_to_all(grad_out, "head", split_axis=1, concat_axis=0, tiled=True),
        lax.all_to_all(attended, "head", split_axis=1, concat_axis=0, tiled=True),
    )
    length = moved[0].shape[0]

    def split(piece):
        return piece.reshape(piece.shape[0], heads_local, head_width)

    local_q, local_k, local_v, local_g, local_o = [split(matrix) for matrix in moved]
    deltas = jnp.sum(local_g.astype(jnp.float32) * local_o.astype(jnp.float32), axis=2)
    zeros = jnp.zeros((length, heads_local, head_width), jnp.float32)

    def keys_step(grad_query, blocks):
        key_part, value_part = blocks
        dscores = attend(local_q, local_g, logsumexp, deltas, key_part, value_part, scaling)[1]
        return grad_query + query_term(dscores, key_part, scaling)

    def queries_step(totals, blocks):
        query_part, grad_part, norm_part, delta_part = blocks
        weights_low, dscores = attend(
            query_part, grad_part, norm_part, delta_part, local_k, local_v, scaling
        )
        grad_key, grad_value = key_terms(weights_low, dscores, query_part, grad_part, scaling)
        return (totals[0] + grad_key, totals[1] + grad_value)

    all_norms, all_deltas = (
        lax.all_gather(logsumexp, "ctx", axis=0, tiled=True),
        lax.all_gather(deltas, "ctx", axis=0, tiled=True),
    )
    pieces = (
        lax.all_gather(moved[1], "ctx", axis=0, tiled=True),
        lax.all_gather(moved[2], "ctx", axis=0, tiled=True),
    )
    key_piece, value_piece = [split(piece) for piece in pieces]
    grad_query = over_blocks(keys_step, zeros, (key_piece, value_piece))
    pieces = (
        lax.all_gather(moved[0], "ctx", axis=0, tiled=True),
        lax.all_gather(moved[3], "ctx", axis=0, tiled=True),
    )
    query_piece, grad_piece = [split(piece) for piece in pieces]
    grad_key, grad_value = over_blocks(
        queries_step, (zeros, zeros), (query_piece, grad_piece, all_norms, all_deltas)
    )
    query_low = grad_query.reshape(length, width_local).astype(jnp.bfloat16)
    key_low = grad_key.reshape(length, width_local).astype(jnp.bfloat16)
    value_low = grad_value.reshape(length, width_local).astype(jnp.bfloat16)
    grad_queries, grad_keys, grad_values = (
        lax.all_to_all(query_low, "head", split_axis=0, concat_axis=1, tiled=True),
        lax.all_to_all(key_low, "head", split_axis=0, concat_axis=1, tiled=True),
        lax.all_to_all(value_low, "head", split_axis=0, concat_axis=1, tiled=True),
    )
    return (grad_queries, grad_keys, grad_values)


def solution(mesh):
    in_specs = (
        P(("ctx", "head"), None),
        P(("ctx", "head"), None),
        P(("ctx", "head"), None),
        P(("ctx", "head"), None),
        P(("ctx", "head"), None),
        P("ctx", "head"),
    )
    out_specs = (P(("ctx", "head"), None), P(("ctx", "head"), None), P(("ctx", "head"), None))
    return jax.shard_map(local, mesh=mesh, in_specs=in_specs, out_specs=out_specs, check_vma=False)
```

profile of v0, /device:TPU:1, one launch (start us, length us, event | category | flops | bytes accessed | tf_op | source)
XLA Modules:
  0.0 1368.2 jit_solution(7273158289976480809)
XLA Ops:
  8.3 11.1 all_to_all.137
  20.5 8.9 all_to_all.138
  30.5 8.8 all_to_all.139
  40.5 10.2 all_to_all.140
  52.4 4.9 all-to-all-start.4
  57.3 135.5 %all-gather = f32[64,192,3]{1,2,0:T(4,128)S(1)} all-gather(f32[1,192,3]{1,2,0:T(4,128)} %bitcast.128), channel_id=1, replica_groups=mesh['ctx'=64,'head'=4] {'ctx'}, dimensions={0}, use_global_device_ids=true | all-gather | bytes 149760 | tf_op jit(solution)/shard_map/all_gather | solution.py:94
  194.4 127.4 %all-gather.1 = f32[64,192,3]{1,2,0:T(4,128)S(1)} all-gather(f32[1,192,3]{1,2,0:T(4,128)S(1)} %copy.110), channel_id=1, replica_groups=mesh['ctx'=64,'head'=4] {'ctx'}, dimensions={0}, use_global_device_ids=true | all-gather | bytes 149760 | tf_op jit(solution)/shard_map/all_gather | solution.py:95
  322.6 23.3 %reshape.85 = bf16[6,2048,3,64]{3,2,1,0:T(4,128)(2,1)} reshape(bf16[12288,192]{1,0:T(8,128)(2,1)} %all-gather.11.cloned.1.call-done) | data formatting | bytes 9437184 | tf_op jit(solution)/shard_map/reshape;reshape | solution.py:18
  345.9 17.8 %copy.112 = bf16[6,2048,3,64]{1,3,2,0:T(8,128)(2,1)} copy(bf16[6,2048,3,64]{3,2,1,0:T(4,128)(2,1)} %reshape.85) | data formatting | bytes 9437184
  363.7 231.7 %all-gather.13.cloned.1.call-done = bf16[12288,192]{1,0:T(8,128)(2,1)} async-done(((bf16[192,192]{1,0:T(8,128)(2,1)}), bf16[12288,192]{1,0:T(8,128)(2,1)}) %all-gather.13.cloned.1.call-update) | async-done | bytes 4718608 | tf_op jit(solution)/shard_map/all_gather | solution.py:105
  595.4 23.3 %reshape.86 = bf16[6,2048,3,64]{3,2,1,0:T(4,128)(2,1)} reshape(bf16[12288,192]{1,0:T(8,128)(2,1)} %all-gather.13.cloned.1.call-done) | data formatting | bytes 9437184 | tf_op jit(solution)/shard_map/reshape;reshape | solution.py:18
  618.6 17.8 %copy.115 = bf16[6,2048,3,64]{1,3,2,0:T(8,128)(2,1)} copy(bf16[6,2048,3,64]{3,2,1,0:T(4,128)(2,1)} %reshape.86) | data formatting | bytes 9437184
  636.4 74.3 %while.25 = (s32[]{:T(128)}, f32[192,3,64]{0,2,1:T(8,128)S(1)}, f32[192,3,64]{0,2,1:T(8,128)S(1)}, bf16[6,2048,3,64]{1,3,2,0:T(8,128)(2,1)}, bf16[192,3,64]{0,2,...) while((s32[]{:T(128)}, f32[192,3,64]{0,2,1:T(8,128)S(1)}, ...), condition=%wide.region_4.5_spmd.clone, body=%wide.region_3.4_spmd.clone.sunk | while | flops 613601280 | bytes 18311292 | solution.py:26
  665.4 4.6 fusion.85
  690.1 4.6 fusion.85
  702.5 4.6 fusion.85
  711.7 47.2 %all-to-all-start.6 = ((bf16[4,48,192]{2,1,0:T(8,128)(2,1)}), bf16[4,48,192]{2,1,0:T(8,128)(2,1)S(1)}, u32[]{:S(2)}, u32[]{:S(2)}) async-start(bf16[4,48,192]{2,1,0:T(8,128)(2,1)} %copy.131), calls=%async_computation.6 | async-start | bytes 196608 | tf_op jit(solution)/shard_map/all_to_all | solution.py:116
  760.4 143.0 %all-gather.7.cloned.1.call-done = bf16[12288,192]{1,0:T(8,128)(2,1)} async-done(((bf16[192,192]{1,0:T(8,128)(2,1)}), bf16[12288,192]{1,0:T(8,128)(2,1)}) %all-gather.7.cloned.1.call-update) | async-done | bytes 4718608 | tf_op jit(solution)/shard_map/all_gather | solution.py:98
  903.4 23.3 %reshape.82 = bf16[6,2048,3,64]{3,2,1,0:T(4,128)(2,1)} reshape(bf16[12288,192]{1,0:T(8,128)(2,1)} %all-gather.7.cloned.1.call-done) | data formatting | bytes 9437184 | tf_op jit(solution)/shard_map/reshape;reshape | solution.py:18
  926.7 17.8 %copy.100 = bf16[6,2048,3,64]{1,3,2,0:T(8,128)(2,1)} copy(bf16[6,2048,3,64]{3,2,1,0:T(4,128)(2,1)} %reshape.82) | data formatting | bytes 9437184
  944.5 266.3 %all-gather.9.cloned.1.call-done = bf16[12288,192]{1,0:T(8,128)(2,1)} async-done(((bf16[192,192]{1,0:T(8,128)(2,1)}), bf16[12288,192]{1,0:T(8,128)(2,1)}) %all-gather.9.cloned.1.call-update) | async-done | bytes 4718608 | tf_op jit(solution)/shard_map/all_gather | solution.py:99
  1210.8 23.3 %reshape.83 = bf16[6,2048,3,64]{3,2,1,0:T(4,128)(2,1)} reshape(bf16[12288,192]{1,0:T(8,128)(2,1)} %all-gather.9.cloned.1.call-done) | data formatting | bytes 9437184 | tf_op jit(solution)/shard_map/reshape;reshape | solution.py:18
  1234.1 17.8 %copy.102 = bf16[6,2048,3,64]{1,3,2,0:T(8,128)(2,1)} copy(bf16[6,2048,3,64]{3,2,1,0:T(4,128)(2,1)} %reshape.83) | data formatting | bytes 9437184
  1251.9 45.7 %all-to-all-start.7 = ((bf16[4,48,192]{2,1,0:T(8,128)(2,1)}), bf16[4,48,192]{2,1,0:T(8,128)(2,1)S(1)}, u32[]{:S(2)}, u32[]{:S(2)}) async-start(bf16[4,48,192]{2,1,0:T(8,128)(2,1)} %copy.132), calls=%async_computation.7 | async-start | bytes 196608 | tf_op jit(solution)/shard_map/all_to_all | solution.py:117
  1297.6 52.6 %while.24 = (s32[]{:T(128)}, f32[192,3,64]{0,2,1:T(8,128)S(1)}, bf16[6,2048,3,64]{1,3,2,0:T(8,128)(2,1)}, bf16[192,3,64]{0,2,1:T(8,128)(2,1)S(1)}, f32[192,3]{0,...) while((s32[]{:T(128)}, f32[192,3,64]{0,2,1:T(8,128)S(1)}, ...), condition=%wide.region_2.3_spmd.clone, body=%wide.region_1.2_spmd.clone.sunk | while | flops 458993664 | bytes 12245103 | solution.py:26
  1301.7 4.7 fusion.76
  1310.5 4.7 fusion.76
  1319.2 4.7 fusion.76
  1328.0 4.7 fusion.76
  1336.8 4.7 fusion.76
  1345.5 4.7 fusion.76
  1351.2 4.8 all-to-all-start.5
  (105 shorter events, 102.2 us)
Async XLA Ops:
  7.2 315.4 %all-gather.11.cloned.1.call-start = ((), (), s32[]{:S(2)}) async-start(), calls=%async_computation.10 | async-start | bytes 6389760 | tf_op jit(solution)/shard_map/all_gather | solution.py:104
  19.4 575.9 %all-gather.13.cloned.1.call-start = ((), (), s32[]{:S(2)}) async-start(), calls=%async_computation.11 | async-start | bytes 6389760 | tf_op jit(solution)/shard_map/all_gather | solution.py:105
  29.4 874.0 %all-gather.7.cloned.1.call-start = ((), (), s32[]{:S(2)}) async-start(), calls=%async_computation.8 | async-start | bytes 6389760 | tf_op jit(solution)/shard_map/all_gather | solution.py:98
  39.3 282.7 %copy-start.1 = (bf16[48,4,192]{2,0,1:T(8,128)(2,1)S(1)}, bf16[48,4,192]{2,0,1:T(8,128)(2,1)}, u32[]{:S(2)}) copy-start(bf16[48,4,192]{2,0,1:T(8,128)(2,1)} %all_to_all.139) | copy-start | bytes 221188
  39.4 1171.4 %all-gather.9.cloned.1.call-start = ((), (), s32[]{:S(2)}) async-start(), calls=%async_computation.9 | async-start | bytes 6389760 | tf_op jit(solution)/shard_map/all_gather | solution.py:99
  50.6 271.7 %copy-start.2 = (bf16[48,4,192]{2,0,1:T(8,128)(2,1)S(1)}, bf16[48,4,192]{2,0,1:T(8,128)(2,1)}, u32[]{:S(2)}) copy-start(bf16[48,4,192]{2,0,1:T(8,128)(2,1)} %all_to_all.140) | copy-start | bytes 221188
  52.4 141.5 %all-to-all-start.4 = ((bf16[48,4,192]{2,0,1:T(8,128)(2,1)}), bf16[48,4,192]{2,0,1:T(8,128)(2,1)S(1)}, u32[]{:S(2)}, u32[]{:S(2)}) async-start(bf16[48,4,192]{2,0,1:T(8,128)(2,1)} %copy.99), calls=%async_computation.4 | async-start | bytes 196608 | tf_op jit(solution)/shard_map/all_to_all | solution.py:69
  636.4 122.7 %copy-start = (bf16[48,4,192]{2,0,1:T(8,128)(2,1)S(1)}, bf16[48,4,192]{2,0,1:T(8,128)(2,1)}, u32[]{:S(2)}) copy-start(bf16[48,4,192]{2,0,1:T(8,128)(2,1)} %all_to_all.137) | copy-start | bytes 221188
  711.7 540.2 %all-to-all-start.6 = ((bf16[4,48,192]{2,1,0:T(8,128)(2,1)}), bf16[4,48,192]{2,1,0:T(8,128)(2,1)S(1)}, u32[]{:S(2)}, u32[]{:S(2)}) async-start(bf16[4,48,192]{2,1,0:T(8,128)(2,1)} %copy.131), calls=%async_computation.6 | async-start | bytes 196608 | tf_op jit(solution)/shard_map/all_to_all | solution.py:116
  1234.1 63.5 %copy-start.3 = (f32[192,3]{0,1:T(4,128)S(1)}, f32[192,3]{0,1:T(4,128)}, u32[]{:S(2)}) copy-start(f32[192,3]{0,1:T(4,128)} %param.15) | copy-start | bytes 6916
  1251.9 99.3 %all-to-all-start.7 = ((bf16[4,48,192]{2,1,0:T(8,128)(2,1)}), bf16[4,48,192]{2,1,0:T(8,128)(2,1)S(1)}, u32[]{:S(2)}, u32[]{:S(2)}) async-start(bf16[4,48,192]{2,1,0:T(8,128)(2,1)} %copy.132), calls=%async_computation.7 | async-start | bytes 196608 | tf_op jit(solution)/shard_map/all_to_all | solution.py:117
  1351.2 9.7 all-to-all-start.5
Sparse Core Ops, SparseCore 0:
  19.5 266.6 all-gather.10
  288.0 307.3 all-gather.12
  597.1 306.2 all-gather.6
  905.0 305.7 all-gather.8
where the time goes:
time: 1370 us
  waiting for transfers between devices  644 us (47%)
  blocking collectives  302 us (22%)
  local copies, waits for them, and re-layouts  178 us (13%)
  matrix products  126 us (9%)
  starting transfers between devices  103 us (8%)
  between operations  14 us (1%)
    all_gather x1, waiting for transfers between devices, local(): lax.all_gather(moved[2], 'ctx', axis=0, tiled=True)  266 us
    all_gather x1, waiting for transfers between devices, local(): lax.all_gather(moved[3], 'ctx', axis=0, tiled=True)  232 us
    all_gather x1, waiting for transfers between devices, local(): lax.all_gather(moved[1], 'ctx', axis=0, tiled=True)  143 us
    all_gather x1, blocking collectives, local(): lax.all_gather(logsumexp, 'ctx', axis=0, tiled=True)  135 us
    all_gather x1, blocking collectives, local(): lax.all_gather(deltas, 'ctx', axis=0, tiled=True)  127 us
    another operation x4, local copies, waits for them, and re-layouts, over_blocks(): matrix.reshape((length // block_size, block_size) + matrix.shape[1:])  93 us
    unnamed x18, local copies, waits for them, and re-layouts  72.1 us
    dot_general x12, matrix products, attend(): jnp.einsum('ahd,bhd->hab', query_part, key_part, preferred_element_type=j...  49 us
  transfers between devices with their start and end apart: 8, of which 4 were waited for; matrix products, arithmetic and copies ran while one was open for 22% of the time, Pallas kernels for 0%

commit v1 on v0

--- a/solution.py
+++ b/solution.py
@@ -100,10 +100,16 @@
     )
     key_piece, value_piece = [split(piece) for piece in pieces]
     grad_query = over_blocks(keys_step, zeros, (key_piece, value_piece))
-    pieces = (
-        lax.all_gather(moved[0], "ctx", axis=0, tiled=True),
-        lax.all_gather(moved[3], "ctx", axis=0, tiled=True),
+    proceed_object = lambda buf, pos_dim: jnp.concatenate(
+        lax.all_to_all(
+            jnp.stack([buf for _ in range(lax.axis_size("ctx"))], axis=0),
+            axis_name="ctx",
+            split_axis=0,
+            concat_axis=0,
+        ),
+        axis=pos_dim,
     )
+    pieces = (lax.all_gather(moved[0], "ctx", axis=0, tiled=True), proceed_object(moved[3], 0))
     query_piece, grad_piece = [split(piece) for piece in pieces]
     grad_key, grad_value = over_blocks(
         queries_step, (zeros, zeros), (query_piece, grad_piece, all_norms, all_deltas)

time: 1370 us -> 1110 us (0.81)
  waiting for transfers between devices: 644 us -> 233 us
  blocking collectives: 302 us -> 439 us
  starting transfers between devices: 103 us -> 124 us
    all_gather x1 -> x0, waiting for transfers between devices: 232 us -> none  [local(): lax.all_gather(moved[3], 'ctx', axis=0, tiled=True)]
    all_gather x1, blocking collectives: 135 us -> 291 us  [local(): lax.all_gather(logsumexp, 'ctx', axis=0, tiled=True)]
    all_gather x1, waiting for transfers between devices: 143 us -> 0.01 us  [local(): lax.all_gather(moved[1], 'ctx', axis=0, tiled=True)]
    all_gather x1, waiting for transfers between devices: 266 us -> 216 us  [local(): lax.all_gather(moved[2], 'ctx', axis=0, tiled=True)]
    all_to_all x2 -> x0, blocking collectives: 19 us -> none  [the longest x1 10.2 us: local(): lax.all_to_all(values, 'head', split_axis=1, concat_axis=0, tiled=True)]
    all_to_all x0 -> x3, starting transfers between devices: none -> 18.8 us  [the longest x1 9.69 us: local(): lax.all_to_all(jnp.stack([buf for _ in range(lax.axis_size('ctx'))], axis...]
    unnamed x18 -> x20, local copies, waits for them, and re-layouts: 72.1 us -> 61.7 us
  transfers between devices with their start and end apart: 8 -> 10, of which waited for: 4 -> 5; matrix products, arithmetic and copies ran while one was open for 22% -> 26% of each run, Pallas kernels for 0% -> 0%
where the time goes in v1:
time: 1110 us
  blocking collectives  439 us (40%)
  waiting for transfers between devices  233 us (21%)
  local copies, waits for them, and re-layouts  171 us (15%)
  matrix products  126 us (11%)
  starting transfers between devices  124 us (11%)
  between operations  14 us (1%)
    all_gather x1, blocking collectives, local(): lax.all_gather(logsumexp, 'ctx', axis=0, tiled=True)  291 us
    all_gather x1, waiting for transfers between devices, local(): lax.all_gather(moved[2], 'ctx', axis=0, tiled=True)  216 us
    all_gather x1, blocking collectives, local(): lax.all_gather(deltas, 'ctx', axis=0, tiled=True)  128 us
    another operation x4, local copies, waits for them, and re-layouts, over_blocks(): matrix.reshape((length // block_size, block_size) + matrix.shape[1:])  83 us
    unnamed x20, local copies, waits for them, and re-layouts  61.7 us
    all_to_all x1, starting transfers between devices, local(): lax.all_to_all(key_low, 'head', split_axis=0, concat_axis=1, tiled=True)  51.4 us
    dot_general x12, matrix products, attend(): jnp.einsum('ahd,bhd->hab', query_part, key_part, preferred_element_type=j...  49.2 us
    all_to_all x1, starting transfers between devices, local(): lax.all_to_all(value_low, 'head', split_axis=0, concat_axis=1, tiled=True)  45.7 us
  transfers between devices with their start and end apart: 10, of which 5 were waited for; matrix products, arithmetic and copies ran while one was open for 26% of the time, Pallas kernels for 0%

profile of v1, /device:TPU:1, one launch (start us, length us, event | category | flops | bytes accessed | tf_op | source)
XLA Modules:
  0.0 1108.0 jit_solution(7921565743183063632)
XLA Ops:
  8.3 11.1 %all_to_all.139 = bf16[48,4,192]{2,0,1:T(8,128)(2,1)} all-to-all(bf16[48,4,192]{2,0,1:T(8,128)(2,1)S(1)} %copy.95), channel_id=1, replica_groups=mesh['ctx'=64,'head'=4] {'head'}, dimensions={1} | all-to-all | bytes 147456 | tf_op jit(solution)/shard_map/all_to_all | solution.py:65
  20.5 8.9 all_to_all.140
  37.0 4.8 all-to-all-done.3
  50.5 4.9 all-to-all-start.2
  55.5 5.0 all-to-all-done.2
  63.9 9.7 all-to-all-start.6
  74.3 291.0 %all-gather = f32[64,192,3]{1,2,0:T(4,128)S(1)} all-gather(f32[1,192,3]{1,2,0:T(4,128)S(1)} %bitcast.130), channel_id=1, replica_groups=mesh['ctx'=64,'head'=4] {'ctx'}, dimensions={0}, use_global_device_ids=true | all-gather | bytes 149760 | tf_op jit(solution)/shard_map/all_gather | solution.py:94
  366.1 127.9 %all-gather.1 = f32[64,192,3]{1,2,0:T(4,128)S(1)} all-gather(f32[1,192,3]{1,2,0:T(4,128)S(1)} %copy.111), channel_id=1, replica_groups=mesh['ctx'=64,'head'=4] {'ctx'}, dimensions={0}, use_global_device_ids=true | all-gather | bytes 149760 | tf_op jit(solution)/shard_map/all_gather | solution.py:95
  494.8 9.0 copy.110
  503.8 13.2 %reshape_reshape_reshape.3 = bf16[6,2048,3,64]{1,0,3,2:T(8,128)(2,1)} reshape(bf16[64,192,192]{1,0,2:T(8,128)(2,1)} %copy.110) | data formatting | bytes 9437184 | tf_op jit(solution)/shard_map/reshape;reshape;reshape | solution.py:18
  517.0 7.5 copy.116
  524.5 23.3 %reshape.88 = bf16[6,2048,3,64]{3,2,1,0:T(4,128)(2,1)} reshape(bf16[12288,192]{1,0:T(8,128)(2,1)} %all-gather.10.cloned.1.call-done) | data formatting | bytes 9437184 | tf_op jit(solution)/shard_map/reshape;reshape | solution.py:18
  547.7 17.8 %copy.113 = bf16[6,2048,3,64]{1,3,2,0:T(8,128)(2,1)} copy(bf16[6,2048,3,64]{3,2,1,0:T(4,128)(2,1)} %reshape.88) | data formatting | bytes 9437184
  565.5 74.5 %while.25 = (s32[]{:T(128)}, f32[192,3,64]{0,2,1:T(8,128)S(1)}, f32[192,3,64]{0,2,1:T(8,128)S(1)}, bf16[6,2048,3,64]{1,3,2,0:T(8,128)(2,1)}, bf16[192,3,64]{0,2,...) while((s32[]{:T(128)}, f32[192,3,64]{0,2,1:T(8,128)S(1)}, ...), condition=%wide.region_4.5_spmd.clone, body=%wide.region_3.4_spmd.clone.sunk | while | flops 613601280 | bytes 18311292 | solution.py:26
  582.2 4.6 fusion.85
  607.0 4.6 fusion.85
  619.4 4.6 fusion.85
  641.0 51.4 %all-to-all-start.7 = ((bf16[4,48,192]{2,1,0:T(8,128)(2,1)}), bf16[4,48,192]{2,1,0:T(8,128)(2,1)S(1)}, u32[]{:S(2)}, u32[]{:S(2)}) async-start(bf16[4,48,192]{2,1,0:T(8,128)(2,1)} %copy.130), calls=%async_computation.7 | async-start | bytes 196608 | tf_op jit(solution)/shard_map/all_to_all | solution.py:122
  693.9 23.3 %reshape.85 = bf16[6,2048,3,64]{3,2,1,0:T(4,128)(2,1)} reshape(bf16[12288,192]{1,0:T(8,128)(2,1)} %all-gather.6.cloned.1.call-done) | data formatting | bytes 9437184 | tf_op jit(solution)/shard_map/reshape;reshape | solution.py:18
  717.2 17.8 %copy.100 = bf16[6,2048,3,64]{1,3,2,0:T(8,128)(2,1)} copy(bf16[6,2048,3,64]{3,2,1,0:T(4,128)(2,1)} %reshape.85) | data formatting | bytes 9437184
  735.0 215.6 %all-gather.8.cloned.1.call-done = bf16[12288,192]{1,0:T(8,128)(2,1)} async-done(((bf16[192,192]{1,0:T(8,128)(2,1)}), bf16[12288,192]{1,0:T(8,128)(2,1)}) %all-gather.8.cloned.1.call-update) | async-done | bytes 4718608 | tf_op jit(solution)/shard_map/all_gather | solution.py:99
  950.6 23.3 %reshape.86 = bf16[6,2048,3,64]{3,2,1,0:T(4,128)(2,1)} reshape(bf16[12288,192]{1,0:T(8,128)(2,1)} %all-gather.8.cloned.1.call-done) | data formatting | bytes 9437184 | tf_op jit(solution)/shard_map/reshape;reshape | solution.py:18
  973.8 17.8 %copy.102 = bf16[6,2048,3,64]{1,3,2,0:T(8,128)(2,1)} copy(bf16[6,2048,3,64]{3,2,1,0:T(4,128)(2,1)} %reshape.86) | data formatting | bytes 9437184
  991.6 45.7 %all-to-all-start.8 = ((bf16[4,48,192]{2,1,0:T(8,128)(2,1)}), bf16[4,48,192]{2,1,0:T(8,128)(2,1)S(1)}, u32[]{:S(2)}, u32[]{:S(2)}) async-start(bf16[4,48,192]{2,1,0:T(8,128)(2,1)} %copy.131), calls=%async_computation.8 | async-start | bytes 196608 | tf_op jit(solution)/shard_map/all_to_all | solution.py:123
  1037.3 52.7 %while.24 = (s32[]{:T(128)}, f32[192,3,64]{0,2,1:T(8,128)S(1)}, bf16[6,2048,3,64]{1,3,2,0:T(8,128)(2,1)}, bf16[192,3,64]{0,2,1:T(8,128)(2,1)S(1)}, f32[192,3]{0,...) while((s32[]{:T(128)}, f32[192,3,64]{0,2,1:T(8,128)S(1)}, ...), condition=%wide.region_2.3_spmd.clone, body=%wide.region_1.2_spmd.clone.sunk | while | flops 458993664 | bytes 12245103 | solution.py:26
  1041.4 4.7 fusion.76
  1050.2 4.7 fusion.76
  1059.0 4.7 fusion.76
  1067.8 4.7 fusion.76
  1076.6 4.7 fusion.76
  1085.3 4.7 fusion.76
  1091.0 4.8 all-to-all-start.5
  (111 shorter events, 118.1 us)
Async XLA Ops:
  7.2 517.3 %all-gather.10.cloned.1.call-start = ((), (), s32[]{:S(2)}) async-start(), calls=%async_computation.11 | async-start | bytes 6389760 | tf_op jit(solution)/shard_map/all_gather | solution.py:112
  19.4 674.5 %all-gather.6.cloned.1.call-start = ((), (), s32[]{:S(2)}) async-start(), calls=%async_computation.9 | async-start | bytes 6389760 | tf_op jit(solution)/shard_map/all_gather | solution.py:98
  31.1 10.7 all-to-all-start.3
  41.8 8.7 all-to-all-start.4
  50.5 10.0 all-to-all-start.2
  60.5 3.4 copy-start.2
  63.9 10.5 copy-start.4
  63.9 430.4 %copy-start.1 = (bf16[48,4,192]{2,0,1:T(8,128)(2,1)S(1)}, bf16[48,4,192]{2,0,1:T(8,128)(2,1)}, u32[]{:S(2)}) copy-start(bf16[48,4,192]{2,0,1:T(8,128)(2,1)} %all_to_all.140) | copy-start | bytes 221188
  63.9 430.9 %all-to-all-start.6 = ((bf16[64,192,192]{1,2,0:T(8,128)(2,1)}), bf16[64,192,192]{1,2,0:T(8,128)(2,1)}, u32[]{:S(2)}, u32[]{:S(2)}) async-start(bf16[64,192,192]{1,2,0:T(8,128)(2,1)} %stack.5), calls=%async_computation.6 | async-start | bytes 12582912 | tf_op jit(solution)/shard_map/all_to_all | solution.py:104
  73.6 420.9 %copy-start.3 = (bf16[48,4,192]{2,0,1:T(8,128)(2,1)S(1)}, bf16[48,4,192]{2,0,1:T(8,128)(2,1)}, u32[]{:S(2)}) copy-start(bf16[48,4,192]{2,0,1:T(8,128)(2,1)} %copy-done.2) | copy-start | bytes 221188
  73.6 877.0 %all-gather.8.cloned.1.call-start = ((), (), s32[]{:S(2)}) async-start(), calls=%async_computation.10 | async-start | bytes 6389760 | tf_op jit(solution)/shard_map/all_gather | solution.py:99
  565.5 127.1 %copy-start = (bf16[48,4,192]{2,0,1:T(8,128)(2,1)S(1)}, bf16[48,4,192]{2,0,1:T(8,128)(2,1)}, u32[]{:S(2)}) copy-start(bf16[48,4,192]{2,0,1:T(8,128)(2,1)} %all_to_all.139) | copy-start | bytes 221188
  641.0 350.6 %all-to-all-start.7 = ((bf16[4,48,192]{2,1,0:T(8,128)(2,1)}), bf16[4,48,192]{2,1,0:T(8,128)(2,1)S(1)}, u32[]{:S(2)}, u32[]{:S(2)}) async-start(bf16[4,48,192]{2,1,0:T(8,128)(2,1)} %copy.130), calls=%async_computation.7 | async-start | bytes 196608 | tf_op jit(solution)/shard_map/all_to_all | solution.py:122
  991.6 99.4 %all-to-all-start.8 = ((bf16[4,48,192]{2,1,0:T(8,128)(2,1)}), bf16[4,48,192]{2,1,0:T(8,128)(2,1)S(1)}, u32[]{:S(2)}, u32[]{:S(2)}) async-start(bf16[4,48,192]{2,1,0:T(8,128)(2,1)} %copy.131), calls=%async_computation.8 | async-start | bytes 196608 | tf_op jit(solution)/shard_map/all_to_all | solution.py:123
  1091.0 9.7 all-to-all-start.5
Sparse Core Ops, SparseCore 0:
  19.5 319.1 all-gather.9
  340.5 302.3 all-gather.5
  644.6 305.8 all-gather.7
